TPU v7x, 128 devices: a whole 4x4x4 slice. The times are simulated.
128 devices in a mesh: wide: 32 (over x, z, core), narrow: 4 (over y).
Axes of the slice: x: 4, y: 4, z: 4, core: 2. Of those that a mesh axis runs over, the one named last changes fastest.
Arguments:
- front: bfloat16 [4, 32, 128, 32, 4, 128], P(None, 'wide', None, None, 'narrow'), may hold values from -6 to 6
- pivot_inverse: bfloat16 [4, 128, 128], replicated, may hold values from -0.0105112052 to 0.17838107
- rhs: bfloat16 [4, 32, 128, 256], P(None, 'wide'), may hold values from -6 to 6
- trail_sol: bfloat16 [4, 32, 128, 256], P(None, 'wide'), may hold values from -1.1953125 to 1.1953125
- block_mask: int32 [4, 32, 32, 4], P(None, 'wide', None, 'narrow'), may hold values 0 or 1
- panel_order: int32 [4], replicated, may hold values from 0 to 3, each once
Outputs:
- front_out: bfloat16 [4, 32, 128, 32, 4, 128], P(None, 'wide', None, None, 'narrow')
- forward_rhs: bfloat16 [4, 32, 128, 256], P(None, 'wide')
- window_solution: bfloat16 [4, 128, 256], replicated
Inputs may be any that keep to these rules, and one draw needn't show every extreme that they name: `panel_order`: each value 0 to 3 appears once.
All inputs are finite; a program needn't handle non-finite values. No bound on the sum of `block_mask` on one device may be relied on, other than what follows from the above.
Results may differ from a plain program's by a relative error of at most 0.0076.
Values may be sent and summed in bfloat16 or wider, within the bound.
No kernel may reach another device: no remote copies, remote signals or barrier semaphores. Data moves between devices by JAX's collectives and lax.ppermute only.
A program may use at most 64 MiB of HBM per device.

v0:
```python
import jax
import jax.numpy as jnp
from jax import lax
from jax.sharding import PartitionSpec as P


def spread(block, axis, source):
    block = jnp.where(lax.axis_index(axis) == source, block, jnp.zeros_like(block))
    return lax.psum(block, axis)


def body(front, pivot_inverse, rhs, trail_sol, block_mask, panel_order):
    rloc = front.shape[0]
    bsize = front.shape[2]
    cloc = front.shape[3]
    nrhs_local = rhs.shape[3]
    panels = panel_order.shape[0]
    nwide = lax.axis_size("wide")
    nnarrow = lax.axis_size("narrow")
    blocks = front.reshape(rloc, bsize, cloc, bsize)
    pattern = block_mask.reshape(rloc, cloc).astype(jnp.float32)
    right = rhs.reshape(rloc, bsize, nrhs_local)
    rows_global = jnp.arange(rloc, dtype=jnp.int32) * nwide + lax.axis_index("wide")
    cols_global = jnp.arange(cloc, dtype=jnp.int32) * nnarrow + lax.axis_index("narrow")
    section_ids = jnp.arange(panels, dtype=jnp.int32)
    rows_rank = jnp.min(
        jnp.where(rows_global[:, None] == panel_order[None, :], section_ids[None, :], panels),
        axis=1,
    )
    cols_rank = jnp.min(
        jnp.where(cols_global[:, None] == panel_order[None, :], section_ids[None, :], panels),
        axis=1,
    )

    def pivot_weight(target):
        return lax.dynamic_index_in_dim(pivot_inverse, target, 0, keepdims=False)

    def panel_factors(col_blocks, row_blocks, target, section):
        weight = pivot_weight(target)
        left = jnp.einsum("rab,bc->rac", col_blocks, weight, preferred_element_type=jnp.float32)
        left = jnp.where((rows_rank > section)[:, None, None], left, 0.0).astype(jnp.bfloat16)
        left = spread(left, "narrow", target % nnarrow)
        upper = jnp.einsum("ac,ajb->cjb", weight, row_blocks, preferred_element_type=jnp.float32)
        upper = jnp.where((cols_rank > section)[None, :, None], upper, 0.0).astype(jnp.bfloat16)
        upper = spread(upper, "wide", target % nwide)
        return (left, upper)

    def column_of(current, target):
        return lax.dynamic_index_in_dim(current, target // nnarrow, 2, keepdims=False)

    def row_of(current, target):
        return lax.dynamic_index_in_dim(current, target // nwide, 0, keepdims=False)

    saved_left = []
    saved_pivot = []
    left, upper = panel_factors(
        column_of(blocks, panel_order[0]), row_of(blocks, panel_order[0]), panel_order[0], 0
    )
    for section in range(panels):
        target = panel_order[section]
        weight = pivot_weight(target)
        product = jnp.einsum("rac,cjb->rajb", left, upper, preferred_element_type=jnp.float32)
        blocks = (blocks.astype(jnp.float32) - pattern[:, None, :, None] * product).astype(
            jnp.bfloat16
        )
        if section + 1 < panels:
            following = panel_order[section + 1]
            next_left, next_upper = panel_factors(
                column_of(blocks, following), row_of(blocks, following), following, section + 1
            )
        pivot_rhs = lax.dynamic_index_in_dim(right, target // nwide, 0, keepdims=False)
        solved = jnp.einsum(
            "ac,an->cn", weight, pivot_rhs, preferred_element_type=jnp.float32
        ).astype(jnp.bfloat16)
        solved = spread(solved, "wide", target % nwide)
        elimination = jnp.einsum("rac,cn->ran", left, solved, preferred_element_type=jnp.float32)
        right = (right.astype(jnp.float32) - elimination).astype(jnp.bfloat16)
        saved_left.append(left)
        saved_pivot.append(solved)
        if section + 1 < panels:
            left, upper = (next_left, next_upper)
    current = trail_sol.reshape(rloc, bsize, nrhs_local)
    window = jnp.zeros((panels, bsize, nrhs_local), jnp.bfloat16)
    for section in reversed(range(panels)):
        target = panel_order[section]
        partial_sum = jnp.einsum(
            "rac,ran->cn", saved_left[section], current, preferred_element_type=jnp.float32
        )
        total = lax.psum(partial_sum, "wide")
        corrected = (saved_pivot[section].astype(jnp.float32) - total).astype(jnp.bfloat16)
        result = jnp.einsum(
            "ac,cn->an", pivot_weight(target), corrected, preferred_element_type=jnp.float32
        ).astype(jnp.bfloat16)
        current = jnp.where((rows_global == target)[:, None, None], result[None], current)
        window = lax.dynamic_update_index_in_dim(window, result, target, 0)
    return (blocks.reshape(front.shape), right.reshape(rhs.shape), window)


def solution(mesh):
    in_specs = (
        P(None, "wide", None, None, "narrow", None),
        P(),
        P(None, "wide", None, None),
        P(None, "wide", None, None),
        P(None, "wide", None, "narrow"),
        P(),
    )
    out_specs = (P(None, "wide", None, None, "narrow", None), P(None, "wide", None, None), P())
    return jax.shard_map(body, mesh=mesh, in_specs=in_specs, out_specs=out_specs, check_vma=False)
```

profile of v0, /device:TPU:1, one launch (start us, length us, event | category | flops | bytes accessed | tf_op | source)
XLA Modules:
  0.0 1070.7 jit_solution(9461470469571352421)
XLA Ops:
  7.2 1.5 fusion.111
  13.5 1.5 constant_dynamic-slice_fusion.1
  16.0 1.3 constant_dynamic-slice_fusion
  18.1 1.6 fusion.2
  24.1 34.5 %all-reduce.17.cloned.1.call-done = bf16[4,128,128]{2,1,0:T(8,128)(2,1)} async-done(((bf16[4,128,128]{2,1,0:T(8,128)(2,1)}), bf16[4,128,128]{2,1,0:T(8,128)(2,1)}) %all-reduce.17.cloned.1.call-update) | async-done | bytes 131088 | tf_op jit(solution)/shard_map/psum | solution.py:9
  58.6 112.0 %all-reduce.39.cloned.1.call-done = (bf16[128,32,128]{2,0,1:T(8,128)(2,1)}, bf16[128,256]{1,0:T(8,128)(2,1)}) async-done(((bf16[128,32,128]{2,0,1:T(8,128)(2,1)}, bf16[128,256]{1,0:T(8,128)(2,1)}), (bf16[128,32,128]{2,0,1:T(8,128)(2,1)}, bf16[128,256]{1,0:T(8,128)(2,1)})) %all-reduce.39.cloned.1.call-update) | async-done | bytes 1114128 | tf_op jit(solution)/shard_map/psum | solution.py:9
  170.6 4.7 fusion
  175.3 2.0 copy-done.2
  178.2 2.7 fusion.3
  185.6 31.7 %all-reduce.19.cloned.1.call-done = bf16[4,128,128]{2,1,0:T(8,128)(2,1)} async-done(((bf16[4,128,128]{2,1,0:T(8,128)(2,1)}), bf16[4,128,128]{2,1,0:T(8,128)(2,1)}) %all-reduce.19.cloned.1.call-update) | async-done | bytes 131088 | tf_op jit(solution)/shard_map/psum | solution.py:9
  217.3 111.8 %all-reduce.37.cloned.1.call-done = (bf16[128,32,128]{2,0,1:T(8,128)(2,1)}, bf16[128,256]{1,0:T(8,128)(2,1)}) async-done(((bf16[128,32,128]{2,0,1:T(8,128)(2,1)}, bf16[128,256]{1,0:T(8,128)(2,1)}), (bf16[128,32,128]{2,0,1:T(8,128)(2,1)}, bf16[128,256]{1,0:T(8,128)(2,1)})) %all-reduce.37.cloned.1.call-update) | async-done | bytes 1114128 | tf_op jit(solution)/shard_map/psum | solution.py:9
  329.1 3.8 subtract_convert_fusion.2
  333.0 2.0 copy-done.1
  335.9 2.7 fusion.4
  343.9 31.0 %all-reduce.21.cloned.1.call-done = bf16[4,128,128]{2,1,0:T(8,128)(2,1)} async-done(((bf16[4,128,128]{2,1,0:T(8,128)(2,1)}), bf16[4,128,128]{2,1,0:T(8,128)(2,1)}) %all-reduce.21.cloned.1.call-update) | async-done | bytes 131088 | tf_op jit(solution)/shard_map/psum | solution.py:9
  374.9 111.8 %all-reduce.35.cloned.1.call-done = (bf16[128,32,128]{2,0,1:T(8,128)(2,1)}, bf16[128,256]{1,0:T(8,128)(2,1)}) async-done(((bf16[128,32,128]{2,0,1:T(8,128)(2,1)}, bf16[128,256]{1,0:T(8,128)(2,1)}), (bf16[128,32,128]{2,0,1:T(8,128)(2,1)}, bf16[128,256]{1,0:T(8,128)(2,1)})) %all-reduce.35.cloned.1.call-update) | async-done | bytes 1114128 | tf_op jit(solution)/shard_map/psum | solution.py:9
  486.7 3.8 subtract_convert_fusion.1
  490.6 2.0 copy-done.3
  493.5 2.7 fusion.5
  496.4 36.1 %all-reduce.23.cloned.1.call-done = bf16[4,128,128]{2,1,0:T(8,128)(2,1)} async-done(((bf16[4,128,128]{2,1,0:T(8,128)(2,1)}), bf16[4,128,128]{2,1,0:T(8,128)(2,1)}) %all-reduce.23.cloned.1.call-update) | async-done | bytes 131088 | tf_op jit(solution)/shard_map/psum | solution.py:9
  532.5 1.9 convolution_bitcast_fusion.3
  536.7 103.3 %all-reduce.25.cloned.1.call-done = f32[128,256]{1,0:T(8,128)} async-done(((f32[128,256]{1,0:T(8,128)}), f32[128,256]{1,0:T(8,128)}) %all-reduce.25.cloned.1.call-update) | async-done | bytes 131088 | tf_op jit(solution)/shard_map/psum | solution.py:89
  639.9 109.0 %all-reduce.33.cloned.1.call-done = (bf16[128,32,128]{2,0,1:T(8,128)(2,1)}, bf16[128,256]{1,0:T(8,128)(2,1)}) async-done(((bf16[128,32,128]{2,0,1:T(8,128)(2,1)}, bf16[128,256]{1,0:T(8,128)(2,1)}), (bf16[128,32,128]{2,0,1:T(8,128)(2,1)}, bf16[128,256]{1,0:T(8,128)(2,1)})) %all-reduce.33.cloned.1.call-update) | async-done | bytes 1114128 | tf_op jit(solution)/shard_map/psum | solution.py:9
  749.0 1.1 bitcast_dynamic-update-slice_fusion.2
  751.6 101.7 %all-reduce.27.cloned.1.call-done = f32[128,256]{1,0:T(8,128)} async-done(((f32[128,256]{1,0:T(8,128)}), f32[128,256]{1,0:T(8,128)}) %all-reduce.27.cloned.1.call-update) | async-done | bytes 131088 | tf_op jit(solution)/shard_map/psum | solution.py:89
  853.3 1.1 bitcast_dynamic-update-slice_fusion.1
  855.5 5.7 fusion.1
  861.3 96.5 %all-reduce.29.cloned.1.call-done = f32[128,256]{1,0:T(8,128)} async-done(((f32[128,256]{1,0:T(8,128)}), f32[128,256]{1,0:T(8,128)}) %all-reduce.29.cloned.1.call-update) | async-done | bytes 131088 | tf_op jit(solution)/shard_map/psum | solution.py:89
  957.7 1.1 bitcast_dynamic-update-slice_fusion
  960.7 6.9 copy.30
  967.6 94.5 %all-reduce.31.cloned.1.call-done = f32[128,256]{1,0:T(8,128)} async-done(((f32[128,256]{1,0:T(8,128)}), f32[128,256]{1,0:T(8,128)}) %all-reduce.31.cloned.1.call-update) | async-done | bytes 131088 | tf_op jit(solution)/shard_map/psum | solution.py:89
  1062.1 1.0 fusion.24
  (79 shorter events, 16.1 us)
Async XLA Ops:
  7.2 7.9 copy-start
  7.2 12.5 %copy-start.9 = (bf16[4,1,128,256]{3,2,1,0:T(8,128)(2,1)S(1)}, bf16[4,1,128,256]{3,2,1,0:T(8,128)(2,1)}, u32[]{:S(2)}) copy-start(bf16[4,1,128,256]{3,2,1,0:T(8,128)(2,1)} %param.8) | copy-start | bytes 786436
  7.2 16.3 %copy-start.15 = (s32[4,1,32,1]{2,3,1,0:T(1,128)S(1)}, s32[4,1,32,1]{2,3,1,0:T(1,128)}, u32[]{:S(2)}) copy-start(s32[4,1,32,1]{2,3,1,0:T(1,128)} %param.10) | copy-start | bytes 1540
  7.2 51.4 %all-reduce.17.cloned.1.call-start = ((), (), s32[]{:S(2)}) async-start(), calls=%async_computation | async-start | bytes 262144 | tf_op jit(solution)/shard_map/psum | solution.py:9
  15.9 154.7 %all-reduce.39.cloned.1.call-start = ((), (), s32[]{:S(2)}) async-start(), calls=%async_computation.11 | async-start | bytes 2228224 | tf_op jit(solution)/shard_map/psum | solution.py:9
  20.5 196.7 %all-reduce.19.cloned.1.call-start = ((), (), s32[]{:S(2)}) async-start(), calls=%async_computation.1 | async-start | bytes 262144 | tf_op jit(solution)/shard_map/psum | solution.py:9
  170.6 10.3 copy-start.7
  170.6 10.3 copy-start.11
  175.3 2.0 copy-start.2
  178.2 150.9 %all-reduce.37.cloned.1.call-start = ((), (), s32[]{:S(2)}) async-start(), calls=%async_computation.10 | async-start | bytes 2228224 | tf_op jit(solution)/shard_map/psum | solution.py:9
  182.0 192.9 %all-reduce.21.cloned.1.call-start = ((), (), s32[]{:S(2)}) async-start(), calls=%async_computation.2 | async-start | bytes 262144 | tf_op jit(solution)/shard_map/psum | solution.py:9
  329.1 9.5 copy-start.8
  329.1 9.5 copy-start.12
  333.0 2.0 copy-start.1
  335.8 150.9 %all-reduce.35.cloned.1.call-start = ((), (), s32[]{:S(2)}) async-start(), calls=%async_computation.9 | async-start | bytes 2228224 | tf_op jit(solution)/shard_map/psum | solution.py:9
  339.6 192.9 %all-reduce.23.cloned.1.call-start = ((), (), s32[]{:S(2)}) async-start(), calls=%async_computation.3 | async-start | bytes 262144 | tf_op jit(solution)/shard_map/psum | solution.py:9
  486.7 9.5 copy-start.4
  486.7 9.5 copy-start.13
  486.7 45.8 %copy-start.6 = (bf16[4,1,128,256]{3,2,1,0:T(8,128)(2,1)S(1)}, bf16[4,1,128,256]{3,2,1,0:T(8,128)(2,1)}, u32[]{:S(2)}) copy-start(bf16[4,1,128,256]{3,2,1,0:T(8,128)(2,1)} %param.9) | copy-start | bytes 786436
  490.6 2.0 copy-start.3
  493.5 146.5 %all-reduce.25.cloned.1.call-start = ((), (), s32[]{:S(2)}) async-start(), calls=%async_computation.4 | async-start | bytes 262144 | tf_op jit(solution)/shard_map/psum | solution.py:89
  532.5 323.0 %copy-start.5 = (bf16[4,128,128]{2,1,0:T(8,128)(2,1)S(1)}, bf16[4,128,128]{2,1,0:T(8,128)(2,1)}, u32[]{:S(2)}) copy-start(bf16[4,128,128]{2,1,0:T(8,128)(2,1)} %all-reduce.23.cloned.1.call-done) | copy-start | bytes 393220
  534.4 214.5 %all-reduce.33.cloned.1.call-start = ((), (), s32[]{:S(2)}) async-start(), calls=%async_computation.8 | async-start | bytes 2228224 | tf_op jit(solution)/shard_map/psum | solution.py:9
  535.3 318.0 %all-reduce.27.cloned.1.call-start = ((), (), s32[]{:S(2)}) async-start(), calls=%async_computation.5 | async-start | bytes 262144 | tf_op jit(solution)/shard_map/psum | solution.py:89
  751.0 206.8 %all-reduce.29.cloned.1.call-start = ((), (), s32[]{:S(2)}) async-start(), calls=%async_computation.6 | async-start | bytes 262144 | tf_op jit(solution)/shard_map/psum | solution.py:89
  855.3 206.8 %all-reduce.31.cloned.1.call-start = ((), (), s32[]{:S(2)}) async-start(), calls=%async_computation.7 | async-start | bytes 262144 | tf_op jit(solution)/shard_map/psum | solution.py:89
  855.5 104.2 %copy-start.14 = (bf16[128,256]{1,0:T(8,128)(2,1)S(1)}, bf16[128,256]{1,0:T(8,128)(2,1)}, u32[]{:S(2)}) copy-start(bf16[128,256]{1,0:T(8,128)(2,1)} %get-tuple-element.13) | copy-start | bytes 196612
  1063.1 0.7 copy-start.10
Sparse Core Ops, SparseCore 0:
  16.0 42.5 all-reduce.16
  62.7 107.9 all-reduce.38
  178.3 38.9 all-reduce.18
  221.1 107.9 all-reduce.36
  335.9 38.8 all-reduce.20
  378.8 107.9 all-reduce.34
  493.6 38.8 all-reduce.22
  536.3 103.5 all-reduce.24
  644.0 104.9 all-reduce.32
  752.6 100.6 all-reduce.26
  857.1 100.6 all-reduce.28
  961.4 100.6 all-reduce.30
where the time goes:
time: 1070 us
  waiting for transfers between devices  974 us (91%)
  matrix products  44.8 us (4%)
  between operations  29.6 us (3%)
  local copies, waits for them, and re-layouts  18 us (2%)
    psum x8, waiting for transfers between devices, spread(): return lax.psum(block, axis)  578 us
    psum x4, waiting for transfers between devices, body(): total = lax.psum(partial_sum, 'wide')  396 us
  transfers between devices with their start and end apart: 12, of which 12 were waited for; matrix products, arithmetic and copies ran while one was open for 3% of the time, Pallas kernels for 0%

commit v1 on v0

--- a/solution.py
+++ b/solution.py
@@ -86,7 +86,9 @@
         partial_sum = jnp.einsum(
             "rac,ran->cn", saved_left[section], current, preferred_element_type=jnp.float32
         )
-        total = lax.psum(partial_sum, "wide")
+        total = partial_sum
+        for hop in (1, 2, 4, 8, 16):
+            total = total + lax.ppermute(total, "wide", [(dev, dev ^ hop) for dev in range(32)])
         corrected = (saved_pivot[section].astype(jnp.float32) - total).astype(jnp.bfloat16)
         result = jnp.einsum(
             "ac,cn->an", pivot_weight(target), corrected, preferred_element_type=jnp.float32

time: 1070 us -> 737 us (0.69)
  waiting for transfers between devices: 974 us -> 607 us
  starting transfers between devices: 0.68 us -> 42.5 us
    psum x4 -> x0, waiting for transfers between devices: 396 us -> none  [body(): total = lax.psum(partial_sum, 'wide')]
    ppermute x0 -> x20, waiting for transfers between devices: none -> 47.5 us  [body(): lax.ppermute(total, 'wide', [(dev, dev ^ hop) for dev in range(32)])]
    ppermute x0 -> x20, starting transfers between devices: none -> 42.2 us  [body(): lax.ppermute(total, 'wide', [(dev, dev ^ hop) for dev in range(32)])]
    psum x8, waiting for transfers between devices: 578 us -> 560 us  [spread(): return lax.psum(block, axis)]
  transfers between devices with their start and end apart: 12 -> 28, of which waited for: 12 -> 26; matrix products, arithmetic and copies ran while one was open for 3% -> 3% of each run, Pallas kernels for 0% -> 0%
where the time goes in v1:
time: 737 us; the launch traced here: 734 us
  waiting for transfers between devices  607 us (82%)
  starting transfers between devices  42.5 us (6%)
  matrix products  35.1 us (5%)
  between operations  29.4 us (4%)
  local copies, waits for them, and re-layouts  15.8 us (2%)
    psum x8, waiting for transfers between devices, spread(): return lax.psum(block, axis)  560 us
    ppermute x20, waiting for transfers between devices, body(): lax.ppermute(total, 'wide', [(dev, dev ^ hop) for dev in range(32)])  47.5 us
    ppermute x20, starting transfers between devices, body(): lax.ppermute(total, 'wide', [(dev, dev ^ hop) for dev in range(32)])  42.2 us
  transfers between devices with their start and end apart: 28, of which 26 were waited for; matrix products, arithmetic and copies ran while one was open for 3% of the time, Pallas kernels for 0%

profile of v1, /device:TPU:1, one launch (start us, length us, event | category | flops | bytes accessed | tf_op | source)
XLA Modules:
  0.0 733.9 jit_solution(11264260198025887327)
XLA Ops:
  24.1 34.5 %all-reduce.13.cloned.1.call-done = bf16[4,128,128]{2,1,0:T(8,128)(2,1)} async-done(((bf16[4,128,128]{2,1,0:T(8,128)(2,1)}), bf16[4,128,128]{2,1,0:T(8,128)(2,1)}) %all-reduce.13.cloned.1.call-update) | async-done | bytes 131088 | tf_op jit(solution)/shard_map/psum | solution.py:9
  58.6 112.0 %all-reduce.27.cloned.1.call-done = (bf16[128,32,128]{2,0,1:T(8,128)(2,1)}, bf16[128,256]{1,0:T(8,128)(2,1)}) async-done(((bf16[128,32,128]{2,0,1:T(8,128)(2,1)}, bf16[128,256]{1,0:T(8,128)(2,1)}), (bf16[128,32,128]{2,0,1:T(8,128)(2,1)}, bf16[128,256]{1,0:T(8,128)(2,1)})) %all-reduce.27.cloned.1.call-update) | async-done | bytes 1114128 | tf_op jit(solution)/shard_map/psum | solution.py:9
  170.6 4.7 fusion
  178.2 2.7 fusion.3
  185.4 31.9 %all-reduce.15.cloned.1.call-done = bf16[4,128,128]{2,1,0:T(8,128)(2,1)} async-done(((bf16[4,128,128]{2,1,0:T(8,128)(2,1)}), bf16[4,128,128]{2,1,0:T(8,128)(2,1)}) %all-reduce.15.cloned.1.call-update) | async-done | bytes 131088 | tf_op jit(solution)/shard_map/psum | solution.py:9
  217.3 111.8 %all-reduce.25.cloned.1.call-done = (bf16[128,32,128]{2,0,1:T(8,128)(2,1)}, bf16[128,256]{1,0:T(8,128)(2,1)}) async-done(((bf16[128,32,128]{2,0,1:T(8,128)(2,1)}, bf16[128,256]{1,0:T(8,128)(2,1)}), (bf16[128,32,128]{2,0,1:T(8,128)(2,1)}, bf16[128,256]{1,0:T(8,128)(2,1)})) %all-reduce.25.cloned.1.call-update) | async-done | bytes 1114128 | tf_op jit(solution)/shard_map/psum | solution.py:9
  329.1 3.8 subtract_convert_fusion.2
  335.9 2.7 fusion.4
  343.8 31.1 %all-reduce.17.cloned.1.call-done = bf16[4,128,128]{2,1,0:T(8,128)(2,1)} async-done(((bf16[4,128,128]{2,1,0:T(8,128)(2,1)}), bf16[4,128,128]{2,1,0:T(8,128)(2,1)}) %all-reduce.17.cloned.1.call-update) | async-done | bytes 131088 | tf_op jit(solution)/shard_map/psum | solution.py:9
  374.9 111.8 %all-reduce.23.cloned.1.call-done = (bf16[128,32,128]{2,0,1:T(8,128)(2,1)}, bf16[128,256]{1,0:T(8,128)(2,1)}) async-done(((bf16[128,32,128]{2,0,1:T(8,128)(2,1)}, bf16[128,256]{1,0:T(8,128)(2,1)}), (bf16[128,32,128]{2,0,1:T(8,128)(2,1)}, bf16[128,256]{1,0:T(8,128)(2,1)})) %all-reduce.23.cloned.1.call-update) | async-done | bytes 1114128 | tf_op jit(solution)/shard_map/psum | solution.py:9
  486.7 3.8 subtract_convert_fusion.1
  496.4 36.1 %all-reduce.19.cloned.1.call-done = bf16[4,128,128]{2,1,0:T(8,128)(2,1)} async-done(((bf16[4,128,128]{2,1,0:T(8,128)(2,1)}), bf16[4,128,128]{2,1,0:T(8,128)(2,1)}) %all-reduce.19.cloned.1.call-update) | async-done | bytes 131088 | tf_op jit(solution)/shard_map/psum | solution.py:9
  533.6 2.8 collective-permute-start
  538.8 3.4 collective-permute-done.1
  542.3 2.9 collective-permute-start.2
  551.6 3.2 collective-permute-start.4
  555.5 90.5 %all-reduce.21.cloned.1.call-done = (bf16[128,32,128]{2,0,1:T(8,128)(2,1)}, bf16[128,256]{1,0:T(8,128)(2,1)}) async-done(((bf16[128,32,128]{2,0,1:T(8,128)(2,1)}, bf16[128,256]{1,0:T(8,128)(2,1)}), (bf16[128,32,128]{2,0,1:T(8,128)(2,1)}, bf16[128,256]{1,0:T(8,128)(2,1)})) %all-reduce.21.cloned.1.call-update) | async-done | bytes 1114128 | tf_op jit(solution)/shard_map/psum | solution.py:9
  649.6 4.2 collective-permute-done.6
  653.8 2.7 collective-permute-start.7
  660.0 3.1 collective-permute-done.8
  663.2 3.2 collective-permute-start.9
  666.9 3.0 collective-permute-done.9
  670.4 3.7 collective-permute-start.10
  675.5 4.4 collective-permute-done.11
  682.2 3.2 collective-permute-done.12
  689.4 3.9 collective-permute-start.14
  693.9 2.8 collective-permute-done.14
  697.2 3.7 collective-permute-start.15
  702.2 4.5 collective-permute-done.16
  707.9 4.2 collective-permute-done.17
  715.1 4.7 copy.38
  719.9 3.9 collective-permute-start.19
  (127 shorter events, 59.2 us)
Async XLA Ops:
  7.2 51.4 %all-reduce.13.cloned.1.call-start = ((), (), s32[]{:S(2)}) async-start(), calls=%async_computation | async-start | bytes 262144 | tf_op jit(solution)/shard_map/psum | solution.py:9
  15.9 154.7 %all-reduce.27.cloned.1.call-start = ((), (), s32[]{:S(2)}) async-start(), calls=%async_computation.7 | async-start | bytes 2228224 | tf_op jit(solution)/shard_map/psum | solution.py:9
  20.5 196.7 %all-reduce.15.cloned.1.call-start = ((), (), s32[]{:S(2)}) async-start(), calls=%async_computation.1 | async-start | bytes 262144 | tf_op jit(solution)/shard_map/psum | solution.py:9
  178.2 150.9 %all-reduce.25.cloned.1.call-start = ((), (), s32[]{:S(2)}) async-start(), calls=%async_computation.6 | async-start | bytes 2228224 | tf_op jit(solution)/shard_map/psum | solution.py:9
  182.0 192.9 %all-reduce.17.cloned.1.call-start = ((), (), s32[]{:S(2)}) async-start(), calls=%async_computation.2 | async-start | bytes 262144 | tf_op jit(solution)/shard_map/psum | solution.py:9
  335.8 150.9 %all-reduce.23.cloned.1.call-start = ((), (), s32[]{:S(2)}) async-start(), calls=%async_computation.5 | async-start | bytes 2228224 | tf_op jit(solution)/shard_map/psum | solution.py:9
  339.7 192.9 %all-reduce.19.cloned.1.call-start = ((), (), s32[]{:S(2)}) async-start(), calls=%async_computation.3 | async-start | bytes 262144 | tf_op jit(solution)/shard_map/psum | solution.py:9
  486.7 45.8 %copy-start.7 = (bf16[4,1,128,256]{3,2,1,0:T(8,128)(2,1)S(1)}, bf16[4,1,128,256]{3,2,1,0:T(8,128)(2,1)}, u32[]{:S(2)}) copy-start(bf16[4,1,128,256]{3,2,1,0:T(8,128)(2,1)} %param.9) | copy-start | bytes 786436
  493.4 152.5 %all-reduce.21.cloned.1.call-start = ((), (), s32[]{:S(2)}) async-start(), calls=%async_computation.4 | async-start | bytes 2228224 | tf_op jit(solution)/shard_map/psum | solution.py:9
  533.6 3.8 collective-permute-start
  537.5 4.8 collective-permute-start.1
  542.3 5.4 collective-permute-start.2
  547.7 3.9 collective-permute-start.3
  551.6 94.3 %collective-permute-start.4 = (f32[128,256]{1,0:T(8,128)S(1)}, f32[128,256]{1,0:T(8,128)S(1)}, u32[]{:S(2)}, u32[]{:S(2)}) collective-permute-start(f32[128,256]{1,0:T(8,128)S(1)} %add.235), channel_id=1, source_target_pairs={{0,64},{4,68},{8,72},{12,76},{16,80},{20,84},{24,88},{28,92},{32,9... | collective-permute-start | bytes 393224 | tf_op jit(solution)/shard_map/ppermute | solution.py:91
  646.0 67.8 %copy-start.2 = (bf16[4,128,32,128]{3,1,2,0:T(8,128)(2,1)S(1)}, bf16[4,128,32,128]{3,1,2,0:T(8,128)(2,1)}, u32[]{:S(2)}) copy-start(bf16[4,128,32,128]{3,1,2,0:T(8,128)(2,1)} %copy-done.1) | copy-start | bytes 12582916
  646.0 67.8 %copy-start.5 = (bf16[4,128,128]{2,1,0:T(8,128)(2,1)S(1)}, bf16[4,128,128]{2,1,0:T(8,128)(2,1)}, u32[]{:S(2)}) copy-start(bf16[4,128,128]{2,1,0:T(8,128)(2,1)} %all-reduce.19.cloned.1.call-done) | copy-start | bytes 393220
  646.0 67.8 %copy-start.8 = (bf16[128,32,128]{2,0,1:T(8,128)(2,1)S(1)}, bf16[128,32,128]{2,0,1:T(8,128)(2,1)}, u32[]{:S(2)}) copy-start(bf16[128,32,128]{2,0,1:T(8,128)(2,1)} %get-tuple-element.12) | copy-start | bytes 3145732
  647.4 1.6 collective-permute-start.5
  649.0 4.8 collective-permute-start.6
  653.8 5.4 collective-permute-start.7
  659.2 3.9 collective-permute-start.8
  663.2 6.8 collective-permute-start.9
  670.4 4.7 collective-permute-start.10
  675.1 4.8 collective-permute-start.11
  679.9 5.4 collective-permute-start.12
  685.3 4.0 collective-permute-start.13
  689.4 7.3 collective-permute-start.14
  697.2 4.7 collective-permute-start.15
  701.9 4.8 collective-permute-start.16
  706.7 5.4 collective-permute-start.17
  712.1 7.7 %collective-permute-start.18 = (f32[128,256]{1,0:T(8,128)S(1)}, f32[128,256]{1,0:T(8,128)S(1)}, u32[]{:S(2)}, u32[]{:S(2)}) collective-permute-start(f32[128,256]{1,0:T(8,128)S(1)} %add.249), channel_id=1, source_target_pairs={{0,32},{4,36},{8,40},{12,44},{16,48},{20,52},{24,56},{28,60},{32,0... | collective-permute-start | bytes 393224 | tf_op jit(solution)/shard_map/ppermute | solution.py:91
  719.9 6.3 collective-permute-start.19
  (14 other events, 110.5 us)
Sparse Core Ops, SparseCore 0:
  16.0 42.5 all-reduce.12
  62.6 107.9 all-reduce.26
  178.3 38.9 all-reduce.14
  221.1 107.9 all-reduce.24
  335.9 38.8 all-reduce.16
  378.7 107.9 all-reduce.22
  493.6 38.8 all-reduce.18
  537.4 108.4 all-reduce.20
